TPU v7x, 256 devices: a whole 4x4x8 slice. The times are simulated.
256 devices in a mesh: seq: 32 (over x, y, core), head: 8 (over z).
Axes of the slice: x: 4, y: 4, z: 8, core: 2. Of those that a mesh axis runs over, the one named last changes fastest.
Arguments:
- projected: bfloat16 [49152, 6912], P(('seq', 'head')), may hold values from -10 to 10
- segment_ids: int32 [49152], replicated, may hold values from 0 to 63, never falling along the last dimension, each value on 1 to 1536 neighbouring positions
- widths: int32 [64], replicated, may hold values from 16 to 64
Outputs:
- attended: bfloat16 [49152, 2304], P(('seq', 'head'))
Inputs may be any that keep to these rules, and one draw needn't show every extreme that they name: `segment_ids`: ids never fall along the sequence; each of the 64 samples covers 1 to 1536 consecutive positions and some sample covers exactly 1536.
All inputs are finite; a program needn't handle non-finite values.
Results may differ from a plain program's by a relative error of at most 0.0088.
Values may be sent and summed in bfloat16 or wider, within the bound.
No kernel may reach another device: no remote copies, remote signals or barrier semaphores. Data moves between devices by JAX's collectives and lax.ppermute only.
A program may use at most 128 MiB of HBM per device.

v0:
```python
import math

import jax
import jax.numpy as jnp
import numpy as np
from jax import lax
from jax.experimental import pallas as pl
from jax.experimental.pallas import tpu as pltpu
from jax.sharding import PartitionSpec as P

D = 2304
HEADS = 24
HD = 96
TOKENS = 49152
SAMPLES = 64
GROUP = 8
SEQ = 32
OWN = 192
SHARD = OWN * GROUP
LANES = 128
SEG_ROWS = TOKENS // LANES
SHARD_ROWS = SHARD // LANES

KV_LANES = 5 * LANES
Q_LANES = 2 * LANES
CODE = 64
BITS = 6
ONE = CODE + 2 * BITS
BIG = float(2**20)
BQ = 2 * OWN
BLOCKS = SHARD // BQ
UNIT = 256
MAX_UNITS = 14
STEPS = (7, 6, 5, 4, 3, 2, 1)
CHUNK = 256
PACK_ROWS = 64
SEG_WINDOW = 24
WINDOW = 3 * SHARD
OUT_ROWS = 2 * OWN + OWN // 4
SCALE = math.log2(math.e) / math.sqrt(HD)


def lane_iota(shape, dtype=jnp.int32):
    return lax.broadcasted_iota(dtype, shape, len(shape) - 1)


def turned(x, amount):
    amount %= LANES
    return x if amount == 0 else pltpu.roll(x, amount, 1)


def id_window(seg_ref, ids_ref, sem):
    first_row = jnp.maximum(device_index() * OWN // LANES - SHARD_ROWS, 0)
    base = pl.multiple_of(jnp.minimum(first_row // 8 * 8, SEG_ROWS - SEG_WINDOW), 8)
    return base, pltpu.make_async_copy(seg_ref.at[pl.ds(base, SEG_WINDOW), :], ids_ref, sem)


def device_index():
    return lax.axis_index("seq") * GROUP + lax.axis_index("head")


def row_copies(x_ref, rows_ref, sems):
    count = OWN // PACK_ROWS
    parts = [pl.ds(i * PACK_ROWS, PACK_ROWS) for i in range(count)]
    return [pltpu.make_async_copy(x_ref.at[p, :], rows_ref.at[p, :], sems.at[i]) for i, p in enumerate(parts)]


def swap_matrix():
    source = lax.broadcasted_iota(jnp.int32, (LANES, LANES), 0)
    target = lane_iota((LANES, LANES))
    partner = jnp.where((target % (HD // 2)) < HD // 4, target + HD // 4, target - HD // 4)
    return jnp.where((source == partner) & (target < HD), 1.0, 0.0).astype(jnp.bfloat16)


def row_tools(rows_ref, at, cos, sin, swap):
    lane = lane_iota((PACK_ROWS, LANES))

    def tile(t):
        return rows_ref[at, t * LANES : (t + 1) * LANES]

    def granules(base, count, target):
        t, g = base // LANES, base % LANES
        value = turned(tile(t), target - g)
        if g + 32 * count > LANES:
            cut = target + LANES - g
            value = jnp.where(lane < cut, value, turned(tile(t + 1), target - g))
        return value

    def rope(base):
        x = granules(base, 3, 0)
        other = jnp.dot(x, swap, preferred_element_type=jnp.float32)
        return (x.astype(jnp.float32) * cos + other * sin).astype(jnp.bfloat16)

    return lane, granules, rope


def pack_kernel(
    x_ref, seg_ref, widths_ref, kv_ref, q_ref, cos_ref, sin_ref, code_ref, rows_ref, ids_ref, wide_ref, row_sems, sems
):
    base, ids_copy = id_window(seg_ref, ids_ref, sems.at[0])
    widths_copy = pltpu.make_async_copy(widths_ref, wide_ref, sems.at[1])
    ids_copy.start()
    widths_copy.start()
    copies = row_copies(x_ref, rows_ref, row_sems)
    for copy in copies:
        copy.start()
    first_tok = device_index() * OWN
    rows = lax.broadcasted_iota(jnp.int32, (OWN, 1), 0)
    lanes = lane_iota((1, LANES))
    freq = jnp.zeros((1, LANES), jnp.float32)
    quarter = HD // 4
    for j in range(quarter):
        freq = jnp.where(lanes % quarter == j, float(np.float32(10000.0 ** (-j / quarter))), freq)
    swap = swap_matrix()
    ids_copy.wait()
    widths_copy.wait()
    own = jnp.zeros((OWN, LANES), jnp.float32)
    window = [(ids_ref[r : r + 1, :].astype(jnp.float32), (base + r) * LANES + lanes - first_tok) for r in range(SEG_WINDOW)]
    for ids, place in window:
        own = own + jnp.where(place == rows, ids, 0.0)
    own = jnp.sum(own, axis=1, keepdims=True)
    before = jnp.zeros((OWN, LANES), jnp.float32)
    for ids, place in window:
        before = before + jnp.where((ids == own) & (place < rows), 1.0, 0.0)
    offset = jnp.sum(before, axis=1, keepdims=True)
    samples = lane_iota((1, SAMPLES)).astype(jnp.float32)
    width = jnp.sum(jnp.where(own == samples, wide_ref[...].astype(jnp.float32), 0.0), axis=1, keepdims=True)
    row_pos = jnp.floor((offset + 0.5) / width)
    col_pos = offset - row_pos * width
    angle = jnp.where(lanes < HD // 2, row_pos, col_pos) * freq
    sine = jnp.sin(angle)
    cos_ref[...] = jnp.cos(angle)
    sin_ref[...] = jnp.where((lanes % (HD // 2)) < quarter, -sine, sine)
    ids = own.astype(jnp.int32)
    shift = jnp.clip(jnp.where(lanes < CODE + BITS, lanes - CODE, lanes - CODE - BITS), 0, BITS - 1)
    bit = (ids >> shift) & 1
    code = jnp.where(lanes < CODE + BITS, 1 - bit, bit)
    code = jnp.where(lanes == ONE, 1, jnp.where((lanes >= CODE) & (lanes < ONE), code, 0))
    code_ref[...] = code.astype(jnp.float32).astype(jnp.bfloat16)
    for copy in copies:
        copy.wait()

    def step(i, carry):
        at = pl.ds(pl.multiple_of(i * PACK_ROWS, PACK_ROWS), PACK_ROWS)
        lane, granules, rope = row_tools(rows_ref, at, cos_ref[at, :], sin_ref[at, :], swap)
        for z in range(GROUP):
            q0 = z * 3 * HD
            k0, v0 = D + q0, 2 * D + q0
            for h in range(3):
                kv_ref[z, at, h * LANES : (h + 1) * LANES] = jnp.where(
                    lane < HD, rope(k0 + h * HD), granules(v0 + 32 * h, 1, HD)
                )
            kv_ref[z, at, 3 * LANES : 4 * LANES] = jnp.where(
                lane < HD, granules(v0 + HD, 3, 0), granules(v0 + 2 * HD, 1, HD)
            )
            q2 = rope(q0 + 2 * HD)
            tail = jnp.where(lane < HD, code_ref[at, :], turned(q2, 32))
            kv_ref[z, at, 4 * LANES : 5 * LANES] = jnp.where(lane < CODE, granules(v0 + 2 * HD + 32, 2, 0), tail)
            q_ref[z, at, :LANES] = jnp.where(lane < HD, rope(q0), turned(q2, HD))
            q_ref[z, at, LANES:] = jnp.where(lane < HD, rope(q0 + HD), turned(q2, 64))
        return carry

    lax.fori_loop(0, OWN // PACK_ROWS, step, 0)


def pack(projected, seg_rows, widths_row):
    vmem, hbm = pl.BlockSpec(memory_space=pltpu.VMEM), pl.BlockSpec(memory_space=pltpu.HBM)
    return pl.pallas_call(
        pack_kernel,
        out_shape=[
            jax.ShapeDtypeStruct((GROUP, OWN, KV_LANES), jnp.bfloat16),
            jax.ShapeDtypeStruct((GROUP, OWN, Q_LANES), jnp.bfloat16),
        ],
        in_specs=[hbm] * 3,
        out_specs=[vmem] * 2,
        scratch_shapes=[
            pltpu.VMEM((OWN, LANES), jnp.float32),
            pltpu.VMEM((OWN, LANES), jnp.float32),
            pltpu.VMEM((OWN, LANES), jnp.bfloat16),
            pltpu.VMEM((OWN, 3 * D), jnp.bfloat16),
            pltpu.VMEM((SEG_WINDOW, LANES), jnp.int32),
            pltpu.VMEM((1, SAMPLES), jnp.int32),
            pltpu.SemaphoreType.DMA((OWN // PACK_ROWS,)),
            pltpu.SemaphoreType.DMA((2,)),
        ],
        compiler_params=pltpu.CompilerParams(vmem_limit_bytes=10 * 1024 * 1024),
        name="pack",
    )(projected, seg_rows, widths_row)


def key_ranges(seg_ref, start_ref, count_ref):
    shard = lax.axis_index("seq")

    def ids_of(index):
        return seg_ref[pl.ds(pl.multiple_of(index * SHARD_ROWS, 4), SHARD_ROWS), :].astype(jnp.float32)

    own_ids = ids_of(shard)
    prev_ids = jnp.where(shard > 0, ids_of(jnp.maximum(shard - 1, 0)), -1.0)
    next_ids = jnp.where(shard < SEQ - 1, ids_of(jnp.minimum(shard + 1, SEQ - 1)), -1.0)
    place = lax.broadcasted_iota(jnp.int32, (SHARD_ROWS, LANES), 0) * LANES + lane_iota((SHARD_ROWS, LANES))

    def total(x):
        return jnp.sum(jnp.sum(x, axis=0, keepdims=True), axis=1, keepdims=True)

    begin, end = WINDOW, 0
    for b in range(BLOCKS):
        first = total(jnp.where(place == b * BQ, own_ids, 0.0))
        last = total(jnp.where(place == b * BQ + BQ - 1, own_ids, 0.0))
        low = total(jnp.where(own_ids < first, 1.0, 0.0) - jnp.where(prev_ids == first, 1.0, 0.0))
        high = total(jnp.where(own_ids <= last, 1.0, 0.0) + jnp.where(next_ids == last, 1.0, 0.0))
        lo, hi = low[0, 0].astype(jnp.int32) + SHARD, high[0, 0].astype(jnp.int32) + SHARD
        start = lo // LANES * LANES
        count = (hi - start + UNIT - 1) // UNIT
        start = jnp.minimum(start, WINDOW - count * UNIT)
        start_ref[b] = start
        count_ref[b] = count
        begin = jnp.minimum(begin, start)
        end = jnp.maximum(end, start + count * UNIT)
    return begin, end


def gather_keys(prev_ref, own_ref, next_ref, seg_ref, kv_ref, v0_ref, start_ref, count_ref):
    begin, end = key_ranges(seg_ref, start_ref, count_ref)
    first_chunk, last_chunk = begin // CHUNK, (end + CHUNK - 1) // CHUNK
    shard_chunks = SHARD // CHUNK

    def copy_from(ref, number):
        low, high = number * shard_chunks, (number + 1) * shard_chunks

        def move(i, carry):
            src = pl.ds(pl.multiple_of((i - low) * CHUNK, CHUNK), CHUNK)
            dst = pl.ds(pl.multiple_of(i * CHUNK, CHUNK), CHUNK)
            lane = lane_iota((CHUNK, LANES))
            parts = []
            for t in range(5):
                value = ref[src, t * LANES : (t + 1) * LANES]
                kv_ref[dst, t * LANES : (t + 1) * LANES] = value
                parts.append(value)
            v0 = jnp.where(lane < 32, turned(parts[0], 32), jnp.where(lane < 64, turned(parts[1], 64), turned(parts[2], 96)))
            v0_ref[dst, :] = jnp.where(lane < HD, v0, jnp.where(lane == HD, 1.0, 0.0).astype(jnp.bfloat16))
            return carry

        lax.fori_loop(jnp.clip(first_chunk, low, high), jnp.clip(last_chunk, low, high), move, 0)

    copy_from(prev_ref, 0)
    copy_from(own_ref, 1)
    copy_from(next_ref, 2)


def attend_kernel(
    prev_ref, own_ref, next_ref, q_ref, seg_ref, out_ref, kv_ref, v0_ref, qa_ref, qc_ref, start_ref, count_ref, *work
):
    gather_keys(prev_ref, own_ref, next_ref, seg_ref, kv_ref, v0_ref, start_ref, count_ref)
    m_refs, o_refs, s_refs = work[:3], work[3:6], work[6:]
    o0_ref, o1_ref, o2_ref = o_refs

    def arrange(b, carry):
        at = pl.ds(pl.multiple_of(b * BQ, BQ), BQ)
        lane = lane_iota((BQ, LANES))
        zero = jnp.zeros((BQ, LANES), jnp.bfloat16)
        t4 = own_ref[at, 4 * LANES :]
        t5 = q_ref[at, :LANES]
        t6 = q_ref[at, LANES:]
        qa_ref[0, at, :] = jnp.where(lane < HD, t5, zero)
        qa_ref[1, at, :] = jnp.where(lane < HD, t6, zero)
        q2 = jnp.where(lane < 32, turned(t5, 32), jnp.where(lane < 64, turned(t6, 64), turned(t4, 96)))
        qa_ref[2, at, :] = jnp.where(lane < HD, q2, zero)
        other = (t4.astype(jnp.float32) - 1.0) * BIG
        qc_ref[at, :] = jnp.where((lane >= CODE) & (lane < ONE), other, 0.0).astype(jnp.bfloat16)
        return carry

    lax.fori_loop(0, BLOCKS, arrange, 0)

    def block(b, carry):
        start, count = start_ref[b], count_ref[b]
        at = pl.ds(pl.multiple_of(b * BQ, BQ), BQ)

        def scores(first_unit, size, j, heads=(0, 1, 2), fresh=False):
            keys = pl.ds(pl.multiple_of(start + first_unit * UNIT + j * size, LANES), size)
            t4 = kv_ref[keys, 4 * LANES :]
            for h in heads:
                k = jnp.concatenate([kv_ref[keys, h * LANES : (h + 1) * LANES], t4], axis=1)
                q = jnp.concatenate([qa_ref[h, at, :], qc_ref[at, :]], axis=1)
                s = lax.dot_general(q, k, (((1,), (1,)), ((), ())), preferred_element_type=jnp.float32)
                for u in range(size // UNIT):
                    s_refs[h][first_unit + j * (size // UNIT) + u] = s[:, u * UNIT : (u + 1) * UNIT]
                top = s[:, :LANES]
                for t in range(1, size // LANES):
                    top = jnp.maximum(top, s[:, t * LANES : (t + 1) * LANES])
                m_refs[h][...] = top if fresh else jnp.maximum(m_refs[h][...], top)

        def blend(first_unit, size, j, heads=(0, 1, 2), fresh=False):
            keys = pl.ds(pl.multiple_of(start + first_unit * UNIT + j * size, LANES), size)
            for h in heads:
                m = jnp.concatenate([m_refs[h][...]] * (UNIT // LANES), axis=1)
                weights = jnp.concatenate(
                    [
                        jnp.exp2(s_refs[h][first_unit + j * (size // UNIT) + u] * SCALE - m).astype(jnp.bfloat16)
                        for u in range(size // UNIT)
                    ],
                    axis=1,
                )
                values = v0_ref[keys, :] if h == 0 else kv_ref[keys, 3 * LANES :]
                blended = jnp.dot(weights, values, preferred_element_type=jnp.float32)
                o_refs[h][...] = blended if fresh else o_refs[h][...] + blended

        def over_keys(what):
            done = 0
            for units in STEPS:
                steps = (count - done) // units
                lax.fori_loop(0, steps, lambda j, c: what(done, units * UNIT, j) or c, 0)
                done = done + steps * units

        def settle(h):
            m_refs[h][...] = jnp.broadcast_to(jnp.max(m_refs[h][...], axis=1, keepdims=True) * SCALE, (BQ, LANES))

        for units in STEPS:

            @pl.when(count == units)
            def _(size=units * UNIT):
                scores(0, size, 0, fresh=True)
                for h in range(3):
                    settle(h)
                blend(0, size, 0, fresh=True)

        @pl.when(count > max(STEPS))
        def _():
            for ref in m_refs:
                ref[...] = jnp.full_like(ref, -3.0e38)
            for ref in o_refs:
                ref[...] = jnp.zeros_like(ref)
            over_keys(scores)
            for h in range(3):
                settle(h)
            over_keys(blend)

        lane = lane_iota((OWN, LANES))
        part = OWN // 4
        part_lane = lane_iota((part, LANES))
        for i in range(BQ // OWN):
            at = slice(i * OWN, (i + 1) * OWN)
            to = b * (BQ // OWN) + i
            o0 = o0_ref[at, :]
            o0 = o0 * (1.0 / o0[:, HD : HD + 1])
            o1 = o1_ref[at, :LANES] * (1.0 / o1_ref[at, LANES:][:, ONE : ONE + 1])
            o2a, o2b = o2_ref[at, :LANES], o2_ref[at, LANES:]
            r2 = 1.0 / o2b[:, ONE : ONE + 1]
            o2a, o2b = o2a * r2, o2b * r2
            out_ref[to, :OWN, :] = jnp.where(lane < HD, o0, o2a).astype(jnp.bfloat16)
            out_ref[to, OWN : 2 * OWN, :] = jnp.where(lane < HD, o1, turned(o2b, 96)).astype(jnp.bfloat16)
            fold = turned(o2b[:part], 96)
            for g in range(1, 4):
                fold = jnp.where(part_lane < 32 * g, fold, turned(o2b[g * part : (g + 1) * part], 32 * g - 32))
            out_ref[to, 2 * OWN :, :] = fold.astype(jnp.bfloat16)
        return carry

    lax.fori_loop(0, BLOCKS, block, 0)


def attend(prev, own, following, queries, seg_rows):
    vmem = pl.BlockSpec(memory_space=pltpu.VMEM)
    return pl.pallas_call(
        attend_kernel,
        out_shape=jax.ShapeDtypeStruct((GROUP, OUT_ROWS, LANES), jnp.bfloat16),
        in_specs=[vmem] * 5,
        out_specs=vmem,
        scratch_shapes=[
            pltpu.VMEM((WINDOW, KV_LANES), jnp.bfloat16),
            pltpu.VMEM((WINDOW, LANES), jnp.bfloat16),
            pltpu.VMEM((3, SHARD, LANES), jnp.bfloat16),
            pltpu.VMEM((SHARD, LANES), jnp.bfloat16),
            pltpu.SMEM((BLOCKS,), jnp.int32),
            pltpu.SMEM((BLOCKS,), jnp.int32),
            *[pltpu.VMEM((BQ, LANES), jnp.float32)] * 4,
            *[pltpu.VMEM((BQ, 2 * LANES), jnp.float32)] * 2,
            *[pltpu.VMEM((MAX_UNITS, BQ, UNIT), jnp.float32)] * 3,
        ],
        compiler_params=pltpu.CompilerParams(vmem_limit_bytes=40 * 1024 * 1024),
        name="attend",
    )(prev, own, following, queries, seg_rows)


def unpack_kernel(in_ref, out_ref):
    lane = lane_iota((OWN, LANES))
    part = OWN // 4

    def source(z, i):
        if i < 3:
            return in_ref[z, :OWN, :], i
        if i < 6:
            return in_ref[z, OWN : 2 * OWN, :], i - 3
        return in_ref[z, (i - 6) * OWN : (i - 5) * OWN, :], 3

    for t in range(D // LANES):
        value = None
        for g in range(4):
            z, i = divmod(4 * t + g, 9)
            if i == 8:
                pieces = [turned(in_ref[z, 2 * OWN :, :], 32 * (g - p)) for p in range(4)]
                moved = jnp.concatenate(pieces, axis=0)
            else:
                tile, at = source(z, i)
                moved = turned(tile, 32 * (g - at))
            value = moved if value is None else jnp.where(lane < 32 * g, value, moved)
        out_ref[:, t * LANES : (t + 1) * LANES] = value


def unpack(returned):
    vmem = pl.BlockSpec(memory_space=pltpu.VMEM)
    return pl.pallas_call(
        unpack_kernel,
        out_shape=jax.ShapeDtypeStruct((OWN, D), jnp.bfloat16),
        in_specs=[vmem],
        out_specs=vmem,
        compiler_params=pltpu.CompilerParams(vmem_limit_bytes=8 * 1024 * 1024),
        name="unpack",
    )(returned)


def body(projected, segment_ids, widths):
    seg_rows = segment_ids.reshape(SEG_ROWS, LANES)
    in_hbm = [pltpu.with_memory_space_constraint(a, pltpu.HBM) for a in (projected, seg_rows, widths.reshape(1, SAMPLES))]
    kv, q = pack(*in_hbm)
    kv = lax.all_to_all(kv, "head", 0, 0, tiled=True)
    kv, q = lax.optimization_barrier((kv, q))
    own = kv.reshape(SHARD, KV_LANES)
    up = [(i, (i + 1) % SEQ) for i in range(SEQ)]
    down = [(j, i) for i, j in up]
    prev = lax.ppermute(own, "seq", up)
    following = lax.ppermute(own, "seq", down)
    q = lax.all_to_all(q, "head", 0, 0, tiled=True)
    out = attend(prev, own, following, q.reshape(SHARD, Q_LANES), seg_rows)
    out = lax.all_to_all(out, "head", 0, 0, tiled=True)
    return unpack(out)


def solution(mesh):
    in_specs = (P(("seq", "head"), None), P(), P())
    out_specs = P(("seq", "head"), None)
    return jax.shard_map(body, mesh=mesh, in_specs=in_specs, out_specs=out_specs, check_vma=False)
```

profile of v0, /device:TPU:15, one launch (start us, length us, event | category | flops | bytes accessed | tf_op | source)
XLA Modules:
  0.0 135.9 jit_solution(11676762993459328805)
XLA Ops:
  0.0 4.9 %pack.1 = (bf16[8,192,640]{2,1,0:T(8,128)(2,1)S(1)}, bf16[8,192,256]{2,1,0:T(8,128)(2,1)S(1)}) custom-call(bf16[192,6912]{1,0:T(8,128)(2,1)} %x_ref.1, s32[384,128]{1,0:T(8,128)} %bitcast.8, s32[1,64]{1,0:T(1,128)} %bitcast.10), custom_call_target="tpu_custom_call" | custom-call | tf_op jit(solution)/shard_map/pack/pallas_call | solution.py:168
  4.9 0.0 copy-start
  4.9 55.4 %all_to_all.15 = bf16[8,192,640]{2,1,0:T(8,128)(2,1)S(1)} all-to-all(bf16[8,192,640]{2,1,0:T(8,128)(2,1)S(1)} %get-tuple-element.9), channel_id=1, replica_groups=mesh['seq'=32,'head'=8] {'head'}, dimensions={0} | all-to-all | bytes 3932160 | tf_op jit(solution)/shard_map/all_to_all | solution.py:424
  60.3 2.0 %collective-permute-start.1 = (bf16[1536,640]{1,0:T(8,128)(2,1)S(1)}, bf16[1536,640]{1,0:T(8,128)(2,1)S(1)}, u32[]{:S(2)}, u32[]{:S(2)}) collective-permute-start(bf16[1536,640]{1,0:T(8,128)(2,1)S(1)} %bitcast.4), channel_id=1, source_target_pairs={{8,0},{16,8},{24,16},{32,24},{40,32},{48,40},{56,48},{64,56},{72,6... | collective-permute-start | bytes 5898248 | tf_op jit(solution)/shard_map/ppermute | solution.py:430
  62.3 1.2 collective-permute-start
  63.5 25.9 %all_to_all.16 = bf16[8,192,256]{2,1,0:T(8,128)(2,1)S(1)} all-to-all(bf16[8,192,256]{2,1,0:T(8,128)(2,1)S(1)} %get-tuple-element.12), channel_id=1, replica_groups=mesh['seq'=32,'head'=8] {'head'}, dimensions={0} | all-to-all | bytes 1572864 | tf_op jit(solution)/shard_map/all_to_all | solution.py:431
  89.4 0.0 collective-permute-done.1.next_ref
  89.4 0.0 collective-permute-done.prev_ref
  89.4 0.0 copy-done
  89.4 17.0 %attend.1 = bf16[8,432,128]{2,1,0:T(8,128)(2,1)S(1)} custom-call(bf16[1536,640]{1,0:T(8,128)(2,1)S(1)} %collective-permute-done.prev_ref, bf16[1536,640]{1,0:T(8,128)(2,1)S(1)} %bitcast.6, bf16[1536,640]{1,0:T(8,128)(2,1)S(1)} %collective-permute-done.1.next_ref, bf16[1536,256]{1,0:T(8,128)(2,1)S(1)} %bitcast.7, s32[384,128]{1,0:T(8,128)S(1)} %bitcast.9), custom_call_target="tpu_custom_call" | custom-call | tf_op jit(solution)/shard_map/attend/pallas_call | solution.py:362
  106.4 28.1 %all_to_all.17.in_ref = bf16[8,432,128]{2,1,0:T(8,128)(2,1)S(1)} all-to-all(bf16[8,432,128]{2,1,0:T(8,128)(2,1)S(1)} %attend.1), channel_id=1, replica_groups=mesh['seq'=32,'head'=8] {'head'}, dimensions={0} | all-to-all | bytes 1769472 | tf_op jit(solution)/shard_map/all_to_all | solution.py:433
  134.4 1.5 %unpack.1 = bf16[192,2304]{1,0:T(8,128)(2,1)} custom-call(bf16[8,432,128]{2,1,0:T(8,128)(2,1)S(1)} %all_to_all.17.in_ref), custom_call_target="tpu_custom_call" | custom-call | tf_op jit(solution)/shard_map/unpack/pallas_call | solution.py:410
Async XLA Ops:
  4.9 84.5 %copy-start = (s32[49152]{0:T(1024)S(1)}, s32[49152]{0:T(1024)}, u32[]{:S(2)}) copy-start(s32[49152]{0:T(1024)} %param.4) | copy-start | bytes 589828
  60.3 29.1 %collective-permute-start.1 = (bf16[1536,640]{1,0:T(8,128)(2,1)S(1)}, bf16[1536,640]{1,0:T(8,128)(2,1)S(1)}, u32[]{:S(2)}, u32[]{:S(2)}) collective-permute-start(bf16[1536,640]{1,0:T(8,128)(2,1)S(1)} %bitcast.4), channel_id=1, source_target_pairs={{8,0},{16,8},{24,16},{32,24},{40,32},{48,40},{56,48},{64,56},{72,6... | collective-permute-start | bytes 5898248 | tf_op jit(solution)/shard_map/ppermute | solution.py:430
  62.3 27.0 %collective-permute-start = (bf16[1536,640]{1,0:T(8,128)(2,1)S(1)}, bf16[1536,640]{1,0:T(8,128)(2,1)S(1)}, u32[]{:S(2)}, u32[]{:S(2)}) collective-permute-start(bf16[1536,640]{1,0:T(8,128)(2,1)S(1)} %bitcast.5), channel_id=1, source_target_pairs={{0,8},{8,16},{16,24},{24,32},{32,40},{40,48},{48,56},{56,64},{64,7... | collective-permute-start | bytes 5898248 | tf_op jit(solution)/shard_map/ppermute | solution.py:429
where the time goes:
time: 136 us
  blocking collectives  109 us (80%)
  Pallas kernels  23.3 us (17%)
  starting transfers between devices  3.19 us (2%)
    all_to_all x1, blocking collectives, body(): kv = lax.all_to_all(kv, 'head', 0, 0, tiled=True)  55.4 us
    all_to_all x1, blocking collectives, body(): out = lax.all_to_all(out, 'head', 0, 0, tiled=True)  28.1 us
    all_to_all x1, blocking collectives, body(): q = lax.all_to_all(q, 'head', 0, 0, tiled=True)  25.9 us
    pallas_call x1, Pallas kernels, attend(): pl.pallas_call(attend_kernel, out_shape=jax.ShapeDtypeStruct((GROUP, OUT_...  17 us
    pallas_call x1, Pallas kernels, pack(): pl.pallas_call(pack_kernel, out_shape=[jax.ShapeDtypeStruct((GROUP, OWN,...  4.87 us
  transfers between devices with their start and end apart: 2, of which 0 were waited for; matrix products, arithmetic and copies ran while one was open for 0% of the time, Pallas kernels for 0%

commit v1 on v0

--- a/solution.py
+++ b/solution.py
@@ -32,7 +32,7 @@
 UNIT = 256
 MAX_UNITS = 14
 STEPS = (7, 6, 5, 4, 3, 2, 1)
-CHUNK = 256
+CHUNK = 512
 PACK_ROWS = 64
 SEG_WINDOW = 24
 WINDOW = 3 * SHARD
@@ -380,7 +380,9 @@
     )(prev, own, following, queries, seg_rows)
 
 
-def unpack_kernel(in_ref, out_ref):
+def unpack_kernel(in_ref, out_hbm, out_ref, sems):
+    group = 3 * LANES
+    copies = []
     lane = lane_iota((OWN, LANES))
     part = OWN // 4
 
@@ -403,6 +405,12 @@
                 moved = turned(tile, 32 * (g - at))
             value = moved if value is None else jnp.where(lane < 32 * g, value, moved)
         out_ref[:, t * LANES : (t + 1) * LANES] = value
+        if (t + 1) * LANES % group == 0:
+            done = pl.ds((t + 1) * LANES - group, group)
+            copies.append(pltpu.make_async_copy(out_ref.at[:, done], out_hbm.at[:, done], sems.at[len(copies)]))
+            copies[-1].start()
+    for copy in copies:
+        copy.wait()
 
 
 def unpack(returned):
@@ -411,7 +419,8 @@
         unpack_kernel,
         out_shape=jax.ShapeDtypeStruct((OWN, D), jnp.bfloat16),
         in_specs=[vmem],
-        out_specs=vmem,
+        out_specs=pl.BlockSpec(memory_space=pltpu.HBM),
+        scratch_shapes=[pltpu.VMEM((OWN, D), jnp.bfloat16), pltpu.SemaphoreType.DMA((D // (3 * LANES),))],
         compiler_params=pltpu.CompilerParams(vmem_limit_bytes=8 * 1024 * 1024),
         name="unpack",
     )(returned)

time: 136 us -> 136 us (level)
  the two profiles are of different devices: /device:TPU:15 before, /device:TPU:20 now
where the time goes in v1:
time: 136 us; the launch traced here: 134 us
  blocking collectives  111 us (82%)
  Pallas kernels  22.6 us (17%)
    all_to_all x1, blocking collectives, body(): kv = lax.all_to_all(kv, 'head', 0, 0, tiled=True)  56.7 us
    all_to_all x1, blocking collectives, body(): out = lax.all_to_all(out, 'head', 0, 0, tiled=True)  27 us
    all_to_all x1, blocking collectives, body(): q = lax.all_to_all(q, 'head', 0, 0, tiled=True)  26.8 us
    pallas_call x1, Pallas kernels, attend(): pl.pallas_call(attend_kernel, out_shape=jax.ShapeDtypeStruct((GROUP, OUT_...  16.4 us
    pallas_call x1, Pallas kernels, pack(): pl.pallas_call(pack_kernel, out_shape=[jax.ShapeDtypeStruct((GROUP, OWN,...  4.91 us
  transfers between devices with their start and end apart: 2, of which 0 were waited for; matrix products, arithmetic and copies ran while one was open for 0% of the time, Pallas kernels for 0%

profile of v1, /device:TPU:20, one launch (start us, length us, event | category | flops | bytes accessed | tf_op | source)
XLA Modules:
  0.0 133.8 jit_solution(1302824265429856923)
XLA Ops:
  0.0 4.9 %pack.1 = (bf16[8,192,640]{2,1,0:T(8,128)(2,1)S(1)}, bf16[8,192,256]{2,1,0:T(8,128)(2,1)S(1)}) custom-call(bf16[192,6912]{1,0:T(8,128)(2,1)} %x_ref.1, s32[384,128]{1,0:T(8,128)} %bitcast.8, s32[1,64]{1,0:T(1,128)} %bitcast.10), custom_call_target="tpu_custom_call" | custom-call | tf_op jit(solution)/shard_map/pack/pallas_call | solution.py:168
  4.9 0.0 copy-start
  4.9 56.7 %all_to_all.15 = bf16[8,192,640]{2,1,0:T(8,128)(2,1)S(1)} all-to-all(bf16[8,192,640]{2,1,0:T(8,128)(2,1)S(1)} %get-tuple-element.9), channel_id=1, replica_groups=mesh['seq'=32,'head'=8] {'head'}, dimensions={0} | all-to-all | bytes 3932160 | tf_op jit(solution)/shard_map/all_to_all | solution.py:433
  61.7 0.0 collective-permute-start.1
  61.7 0.5 collective-permute-start
  62.2 26.8 %all_to_all.16 = bf16[8,192,256]{2,1,0:T(8,128)(2,1)S(1)} all-to-all(bf16[8,192,256]{2,1,0:T(8,128)(2,1)S(1)} %get-tuple-element.12), channel_id=1, replica_groups=mesh['seq'=32,'head'=8] {'head'}, dimensions={0} | all-to-all | bytes 1572864 | tf_op jit(solution)/shard_map/all_to_all | solution.py:440
  89.0 0.0 collective-permute-done.1.next_ref
  89.0 0.0 collective-permute-done.prev_ref
  89.0 0.0 copy-done
  89.0 16.4 %attend.1 = bf16[8,432,128]{2,1,0:T(8,128)(2,1)S(1)} custom-call(bf16[1536,640]{1,0:T(8,128)(2,1)S(1)} %collective-permute-done.prev_ref, bf16[1536,640]{1,0:T(8,128)(2,1)S(1)} %bitcast.6, bf16[1536,640]{1,0:T(8,128)(2,1)S(1)} %collective-permute-done.1.next_ref, bf16[1536,256]{1,0:T(8,128)(2,1)S(1)} %bitcast.7, s32[384,128]{1,0:T(8,128)S(1)} %bitcast.9), custom_call_target="tpu_custom_call" | custom-call | tf_op jit(solution)/shard_map/attend/pallas_call | solution.py:362
  105.4 27.0 %all_to_all.17.in_ref = bf16[8,432,128]{2,1,0:T(8,128)(2,1)S(1)} all-to-all(bf16[8,432,128]{2,1,0:T(8,128)(2,1)S(1)} %attend.1), channel_id=1, replica_groups=mesh['seq'=32,'head'=8] {'head'}, dimensions={0} | all-to-all | bytes 1769472 | tf_op jit(solution)/shard_map/all_to_all | solution.py:442
  132.4 1.3 unpack.1
Async XLA Ops:
  4.9 84.1 %copy-start = (s32[49152]{0:T(1024)S(1)}, s32[49152]{0:T(1024)}, u32[]{:S(2)}) copy-start(s32[49152]{0:T(1024)} %param.4) | copy-start | bytes 589828
  61.7 27.3 %collective-permute-start.1 = (bf16[1536,640]{1,0:T(8,128)(2,1)S(1)}, bf16[1536,640]{1,0:T(8,128)(2,1)S(1)}, u32[]{:S(2)}, u32[]{:S(2)}) collective-permute-start(bf16[1536,640]{1,0:T(8,128)(2,1)S(1)} %bitcast.4), channel_id=1, source_target_pairs={{8,0},{16,8},{24,16},{32,24},{40,32},{48,40},{56,48},{64,56},{72,6... | collective-permute-start | bytes 5898248 | tf_op jit(solution)/shard_map/ppermute | solution.py:439
  61.7 27.3 %collective-permute-start = (bf16[1536,640]{1,0:T(8,128)(2,1)S(1)}, bf16[1536,640]{1,0:T(8,128)(2,1)S(1)}, u32[]{:S(2)}, u32[]{:S(2)}) collective-permute-start(bf16[1536,640]{1,0:T(8,128)(2,1)S(1)} %bitcast.5), channel_id=1, source_target_pairs={{0,8},{8,16},{16,24},{24,32},{32,40},{40,48},{48,56},{56,64},{64,7... | collective-permute-start | bytes 5898248 | tf_op jit(solution)/shard_map/ppermute | solution.py:438

commit v2 on v1

--- a/solution.py
+++ b/solution.py
@@ -199,16 +199,21 @@
     next_ids = jnp.where(shard < SEQ - 1, ids_of(jnp.minimum(shard + 1, SEQ - 1)), -1.0)
     place = lax.broadcasted_iota(jnp.int32, (SHARD_ROWS, LANES), 0) * LANES + lane_iota((SHARD_ROWS, LANES))
 
-    def total(x):
-        return jnp.sum(jnp.sum(x, axis=0, keepdims=True), axis=1, keepdims=True)
-
+    def totals(xs):
+        return jnp.sum(jnp.concatenate([jnp.sum(x, axis=0, keepdims=True) for x in xs], axis=0), axis=1, keepdims=True)
+
+    spots = [at for b in range(BLOCKS) for at in (b * BQ, b * BQ + BQ - 1)]
+    ids = totals([jnp.where(place == at, own_ids, 0.0) for at in spots])
+    ends = []
+    for b in range(BLOCKS):
+        first, last = ids[2 * b : 2 * b + 1], ids[2 * b + 1 : 2 * b + 2]
+        ends.append(jnp.where(own_ids < first, 1.0, 0.0) - jnp.where(prev_ids == first, 1.0, 0.0))
+        ends.append(jnp.where(own_ids <= last, 1.0, 0.0) + jnp.where(next_ids == last, 1.0, 0.0))
+    ends = totals(ends)
     begin, end = WINDOW, 0
     for b in range(BLOCKS):
-        first = total(jnp.where(place == b * BQ, own_ids, 0.0))
-        last = total(jnp.where(place == b * BQ + BQ - 1, own_ids, 0.0))
-        low = total(jnp.where(own_ids < first, 1.0, 0.0) - jnp.where(prev_ids == first, 1.0, 0.0))
-        high = total(jnp.where(own_ids <= last, 1.0, 0.0) + jnp.where(next_ids == last, 1.0, 0.0))
-        lo, hi = low[0, 0].astype(jnp.int32) + SHARD, high[0, 0].astype(jnp.int32) + SHARD
+        lo = ends[2 * b, 0].astype(jnp.int32) + SHARD
+        hi = ends[2 * b + 1, 0].astype(jnp.int32) + SHARD
         start = lo // LANES * LANES
         count = (hi - start + UNIT - 1) // UNIT
         start = jnp.minimum(start, WINDOW - count * UNIT)

time: 136 us -> 136 us (level)
    all_to_all x1, blocking collectives: 27 us -> 28.7 us  [body(): out = lax.all_to_all(out, 'head', 0, 0, tiled=True)]
where the time goes in v2:
time: 136 us; the launch traced here: 135 us
  blocking collectives  112 us (82%)
  Pallas kernels  21.9 us (16%)
    all_to_all x1, blocking collectives, body(): kv = lax.all_to_all(kv, 'head', 0, 0, tiled=True)  56.7 us
    all_to_all x1, blocking collectives, body(): out = lax.all_to_all(out, 'head', 0, 0, tiled=True)  28.7 us
    all_to_all x1, blocking collectives, body(): q = lax.all_to_all(q, 'head', 0, 0, tiled=True)  26.8 us
    pallas_call x1, Pallas kernels, attend(): pl.pallas_call(attend_kernel, out_shape=jax.ShapeDtypeStruct((GROUP, OUT_...  15.7 us
    pallas_call x1, Pallas kernels, pack(): pl.pallas_call(pack_kernel, out_shape=[jax.ShapeDtypeStruct((GROUP, OWN,...  4.91 us
  transfers between devices with their start and end apart: 2, of which 0 were waited for; matrix products, arithmetic and copies ran while one was open for 0% of the time, Pallas kernels for 0%

profile of v2, /device:TPU:20, one launch (start us, length us, event | category | flops | bytes accessed | tf_op | source)
XLA Modules:
  0.0 134.9 jit_solution(14326115721932011504)
XLA Ops:
  0.0 4.9 %pack.1 = (bf16[8,192,640]{2,1,0:T(8,128)(2,1)S(1)}, bf16[8,192,256]{2,1,0:T(8,128)(2,1)S(1)}) custom-call(bf16[192,6912]{1,0:T(8,128)(2,1)} %x_ref.1, s32[384,128]{1,0:T(8,128)} %bitcast.8, s32[1,64]{1,0:T(1,128)} %bitcast.10), custom_call_target="tpu_custom_call" | custom-call | tf_op jit(solution)/shard_map/pack/pallas_call | solution.py:168
  4.9 0.0 copy-start
  4.9 56.7 %all_to_all.15 = bf16[8,192,640]{2,1,0:T(8,128)(2,1)S(1)} all-to-all(bf16[8,192,640]{2,1,0:T(8,128)(2,1)S(1)} %get-tuple-element.9), channel_id=1, replica_groups=mesh['seq'=32,'head'=8] {'head'}, dimensions={0} | all-to-all | bytes 3932160 | tf_op jit(solution)/shard_map/all_to_all | solution.py:438
  61.7 0.0 collective-permute-start.1
  61.7 0.5 collective-permute-start
  62.2 26.8 %all_to_all.16 = bf16[8,192,256]{2,1,0:T(8,128)(2,1)S(1)} all-to-all(bf16[8,192,256]{2,1,0:T(8,128)(2,1)S(1)} %get-tuple-element.12), channel_id=1, replica_groups=mesh['seq'=32,'head'=8] {'head'}, dimensions={0} | all-to-all | bytes 1572864 | tf_op jit(solution)/shard_map/all_to_all | solution.py:445
  89.0 0.0 collective-permute-done.1.next_ref
  89.0 0.0 collective-permute-done.prev_ref
  89.0 0.0 copy-done
  89.0 15.7 %attend.1 = bf16[8,432,128]{2,1,0:T(8,128)(2,1)S(1)} custom-call(bf16[1536,640]{1,0:T(8,128)(2,1)S(1)} %collective-permute-done.prev_ref, bf16[1536,640]{1,0:T(8,128)(2,1)S(1)} %bitcast.6, bf16[1536,640]{1,0:T(8,128)(2,1)S(1)} %collective-permute-done.1.next_ref, bf16[1536,256]{1,0:T(8,128)(2,1)S(1)} %bitcast.7, s32[384,128]{1,0:T(8,128)S(1)} %bitcast.9), custom_call_target="tpu_custom_call" | custom-call | tf_op jit(solution)/shard_map/attend/pallas_call | solution.py:367
  104.7 28.7 %all_to_all.17.in_ref = bf16[8,432,128]{2,1,0:T(8,128)(2,1)S(1)} all-to-all(bf16[8,432,128]{2,1,0:T(8,128)(2,1)S(1)} %attend.1), channel_id=1, replica_groups=mesh['seq'=32,'head'=8] {'head'}, dimensions={0} | all-to-all | bytes 1769472 | tf_op jit(solution)/shard_map/all_to_all | solution.py:447
  133.4 1.3 unpack.1
Async XLA Ops:
  4.9 84.1 %copy-start = (s32[49152]{0:T(1024)S(1)}, s32[49152]{0:T(1024)}, u32[]{:S(2)}) copy-start(s32[49152]{0:T(1024)} %param.4) | copy-start | bytes 589828
  61.7 27.3 %collective-permute-start.1 = (bf16[1536,640]{1,0:T(8,128)(2,1)S(1)}, bf16[1536,640]{1,0:T(8,128)(2,1)S(1)}, u32[]{:S(2)}, u32[]{:S(2)}) collective-permute-start(bf16[1536,640]{1,0:T(8,128)(2,1)S(1)} %bitcast.4), channel_id=1, source_target_pairs={{8,0},{16,8},{24,16},{32,24},{40,32},{48,40},{56,48},{64,56},{72,6... | collective-permute-start | bytes 5898248 | tf_op jit(solution)/shard_map/ppermute | solution.py:444
  61.7 27.3 %collective-permute-start = (bf16[1536,640]{1,0:T(8,128)(2,1)S(1)}, bf16[1536,640]{1,0:T(8,128)(2,1)S(1)}, u32[]{:S(2)}, u32[]{:S(2)}) collective-permute-start(bf16[1536,640]{1,0:T(8,128)(2,1)S(1)} %bitcast.5), channel_id=1, source_target_pairs={{0,8},{8,16},{16,24},{24,32},{32,40},{40,48},{48,56},{56,64},{64,7... | collective-permute-start | bytes 5898248 | tf_op jit(solution)/shard_map/ppermute | solution.py:443
